TPU v7x, 256 devices: a whole 4x4x8 slice. The times are simulated.
256 devices in a mesh: trav: 8 (over z), bulk: 32 (over y, x, core).
Axes of the slice: x: 4, y: 4, z: 8, core: 2. Of those that a mesh axis runs over, the one named last changes fastest.
Arguments:
- parents: bfloat16 [49152, 1024], P(('trav', 'bulk')), may hold values from -6 to 6
- act_table: bfloat16 [128, 1024], replicated, may hold values from -5 to 5
- bucket_table: bfloat16 [8192, 1024], P('bulk'), may hold values from -5 to 5
- w_first: bfloat16 [1024, 2048], P(('trav', 'bulk')), may hold values from -0.1875 to 0.1875
- b_first: float32 [2048], replicated, may hold values from -3 to 3
- w_second: bfloat16 [2048, 2048], P(('trav', 'bulk')), may hold values from -0.1875 to 0.1875
- b_second: float32 [2048], replicated, may hold values from -3 to 3
- w_head: bfloat16 [2048, 8], replicated, may hold values from -0.1875 to 0.1875
- b_head: float32 [8], replicated, may hold values from -3 to 3
- branch_counts: int32 [49152], P(('trav', 'bulk')), may hold values from 1 to 4
- sampled_actions: int32 [49152, 4], P(('trav', 'bulk')), may hold values from 0 to 127
- bucket_owner: int32 [49152, 1], P(('trav', 'bulk')), may hold values from 0 to 31; in each aligned block of 192 rows (0 to 191, 192 to 383, ...) at most 8 rows name the same one
- bucket_row: int32 [49152], P(('trav', 'bulk')), may hold values from 0 to 255
- legal_mask: int32 [49152, 32], P(('trav', 'bulk')), may hold values 0 or 1
- ancestor: int32 [49152], P(('trav', 'bulk')), may hold values from 0 to 47
Outputs:
- strategy: float32 [49152, 32], P(('trav', 'bulk'))
- ancestor_value: float32 [12288], P(('trav', 'bulk'))
Inputs may be any that keep to these rules, and one draw needn't show every extreme that they name: `bucket_owner`: in each aligned block of 192 histories (the histories of one device) no evaluator is named more than 8 times, a bound that some block reaches.
All inputs are finite; a program needn't handle non-finite values. No bound on the sum of `legal_mask` on one device may be relied on, other than what follows from the above.
Results may differ from a plain program's by a relative error of at most 0.0078.
Values may be sent and summed in bfloat16 or wider, within the bound.
A program may use at most 64 MiB of HBM per device.

v0:
```python
import jax
import jax.numpy as jnp
from jax import lax
from jax.sharding import PartitionSpec as P

tremble = 0.05


def network(inputs, w_first, b_first, w_second, b_second, w_head, b_head):
    columns = inputs
    first = jnp.dot(
        columns,
        lax.all_gather(w_first, ("trav", "bulk"), axis=0, tiled=True),
        preferred_element_type=jnp.float32,
    )
    hidden_one = jnp.maximum(first + b_first, 0.0).astype(jnp.bfloat16)
    columns = hidden_one
    second = jnp.dot(
        columns,
        lax.all_gather(w_second, ("trav", "bulk"), axis=0, tiled=True),
        preferred_element_type=jnp.float32,
    )
    hidden_two = jnp.maximum(second + b_second, 0.0).astype(jnp.bfloat16)
    return jnp.dot(hidden_two, w_head, preferred_element_type=jnp.float32) + b_head


def body(
    parents,
    act_table,
    bucket_table,
    w_first,
    b_first,
    w_second,
    b_second,
    w_head,
    b_head,
    branch_counts,
    sampled_actions,
    bucket_owner,
    bucket_row,
    legal_mask,
    ancestor,
):
    par_count = parents.shape[0]
    feature_count = parents.shape[1]
    branch_slots = sampled_actions.shape[1]
    vocab_size = act_table.shape[0]
    action_count = w_head.shape[1]
    bulk_count = lax.axis_size("bulk")
    capacity = max(2, (4 * par_count + 3 * bulk_count - 1) // (3 * bulk_count))
    slot_total = bulk_count * capacity
    action_onehot = (
        sampled_actions.reshape(-1)[:, None] == jnp.arange(vocab_size)[None, :]
    ).astype(jnp.bfloat16)
    act_rows = jnp.dot(action_onehot, act_table, preferred_element_type=jnp.float32)
    base = (jnp.repeat(parents.astype(jnp.float32), branch_slots, axis=0) + act_rows).astype(
        jnp.bfloat16
    )
    base = lax.optimization_barrier(base)
    owner_index = bucket_owner[:, 0]
    owner_hits = (owner_index[:, None] == jnp.arange(bulk_count)[None, :]).astype(jnp.int32)
    earlier = jnp.cumsum(owner_hits, axis=0) - owner_hits
    slot_index = owner_index * capacity + jnp.sum(earlier * owner_hits, axis=1)
    placement_int = (slot_index[None, :] == jnp.arange(slot_total)[:, None]).astype(jnp.int32)
    slot_bucket = jnp.sum(placement_int * bucket_row[None, :], axis=1).reshape(bulk_count, capacity)
    placement = placement_int.astype(jnp.bfloat16)
    outgoing = jnp.dot(
        placement,
        base.reshape(par_count, branch_slots * feature_count),
        preferred_element_type=jnp.float32,
    )
    outgoing = outgoing.astype(jnp.bfloat16).reshape(
        bulk_count, capacity * branch_slots, feature_count
    )
    arrived_rows = lax.all_to_all(outgoing, "bulk", split_axis=0, concat_axis=0, tiled=True)
    arrived_ids = lax.all_to_all(slot_bucket, "bulk", split_axis=0, concat_axis=0, tiled=True)
    table_rows = jnp.take(bucket_table, arrived_ids.reshape(-1), axis=0)
    inputs = (
        arrived_rows.reshape(slot_total, branch_slots, feature_count).astype(jnp.float32)
        + table_rows.astype(jnp.float32)[:, None, :]
    )
    inputs = inputs.astype(jnp.bfloat16).reshape(slot_total * branch_slots, feature_count)
    evaluated = network(inputs, w_first, b_first, w_second, b_second, w_head, b_head)
    returned = lax.all_to_all(
        evaluated.reshape(bulk_count, capacity * branch_slots * action_count).astype(jnp.bfloat16),
        "bulk",
        split_axis=0,
        concat_axis=0,
        tiled=True,
    ).astype(jnp.float32)
    advantage = jnp.take(
        returned.reshape(slot_total, branch_slots * action_count), slot_index, axis=0
    )
    advantage = advantage.reshape(par_count, branch_slots, action_count)
    first_action = (jnp.arange(action_count) == 0).astype(jnp.float32)
    allowed = jnp.maximum(
        legal_mask.reshape(par_count, branch_slots, action_count).astype(jnp.float32), first_action
    )
    positive = allowed * (jnp.maximum(advantage, 0.0) + tremble)
    sigma = positive / jnp.sum(positive, axis=-1, keepdims=True)
    live = (jnp.arange(branch_slots)[None, :] < branch_counts[:, None]).astype(jnp.float32)
    strategy = (sigma * live[:, :, None]).reshape(par_count, branch_slots * action_count)
    branch_value = jnp.sum(sigma * advantage, axis=-1)
    history_value = jnp.sum(branch_value * live, axis=1) / branch_counts.astype(jnp.float32)
    node_count = par_count // 4
    node_onehot = (ancestor[:, None] == jnp.arange(node_count)[None, :]).astype(jnp.float32)
    ancestor_value = jnp.sum(node_onehot * history_value[:, None], axis=0)
    return (strategy, ancestor_value)


def solution(mesh):
    return jax.shard_map(
        body,
        mesh=mesh,
        in_specs=(
            P(("trav", "bulk"), None),
            P(),
            P("bulk", None),
            P(("trav", "bulk"), None),
            P(),
            P(("trav", "bulk"), None),
            P(),
            P(),
            P(),
            P(("trav", "bulk")),
            P(("trav", "bulk"), None),
            P(("trav", "bulk"), None),
            P(("trav", "bulk")),
            P(("trav", "bulk"), None),
            P(("trav", "bulk")),
        ),
        out_specs=(P(("trav", "bulk"), None), P(("trav", "bulk"))),
        check_vma=False,
    )
```

profile of v0, /device:TPU:1, one launch (start us, length us, event | category | flops | bytes accessed | tf_op | source)
XLA Modules:
  0.0 301.7 jit_solution(12102274634874806539)
XLA Ops:
  7.2 0.7 all-gather.6.cloned.1.call-update
  8.0 0.7 all-gather.4.cloned.1.call-update
  8.7 0.7 iota_compare_fusion.4
  9.4 0.6 reduce-window.6
  10.0 0.2 slice_reduce_fusion
  10.2 0.1 bitcast_bitcast_fusion
  10.3 0.7 fusion.12
  11.0 0.7 multiply_add_fusion
  11.7 0.8 select_reduce_fusion
  12.5 0.7 all_to_all.14
  13.2 8.6 %all-to-all-start.1 = ((s32[32,1,8]{2,1,0:T(1,128)}), s32[32,1,8]{2,1,0:T(1,128)S(1)}, u32[]{:S(2)}, u32[]{:S(2)}) async-start(s32[32,1,8]{2,1,0:T(1,128)} %bitcast.4), calls=%async_computation.1 | async-start | bytes 32768 | tf_op jit(solution)/shard_map/all_to_all | solution.py:76
  21.8 3.5 %broadcast_in_dim.48 = f32[192,4,1024]{2,1,0:T(4,128)} broadcast(bf16[192,1024]{1,0:T(8,128)(2,1)} %param.15), dimensions={0,2} | broadcast | bytes 3538944 | tf_op jit(solution)/shard_map/broadcast_in_dim | solution.py:56
  25.3 5.0 %reshape.171 = f32[768,1024]{1,0:T(8,128)} reshape(f32[192,4,1024]{2,1,0:T(4,128)} %broadcast_in_dim.48) | data formatting | bytes 6291456 | tf_op jit(solution)/shard_map/reshape | solution.py:56
  30.3 0.1 copy.55
  30.4 0.1 eq.83
  30.6 2.5 add_convert_fusion
  33.1 2.3 reshape.172
  35.3 2.2 convolution_convert_fusion
  37.6 2.6 reshape.173
  40.2 7.4 %all-to-all-start = ((bf16[32,32,1024]{2,1,0:T(8,128)(2,1)}), bf16[32,32,1024]{2,1,0:T(8,128)(2,1)S(1)}, u32[]{:S(2)}, u32[]{:S(2)}) async-start(bf16[32,32,1024]{2,1,0:T(8,128)(2,1)} %reshape.173), calls=%async_computation | async-start | bytes 4194304 | tf_op jit(solution)/shard_map/all_to_all | solution.py:75
  47.6 0.1 reshape.175
  47.7 0.5 broadcast.149
  48.2 0.7 reduce.11
  48.9 0.1 reshape.174
  49.1 1.2 gather_fusion
  50.3 0.1 select_convert_fusion
  50.4 3.1 %add.100 = f32[256,4,1024]{2,1,0:T(4,128)} broadcast(f32[256,1024]{1,0:T(8,128)S(1)} %select_convert_fusion), dimensions={0,2} | broadcast | bytes 5242880 | tf_op jit(solution)/shard_map/add | solution.py:79
  53.5 5.3 %add.101 = f32[1024,1024]{1,0:T(8,128)} reshape(f32[256,4,1024]{2,1,0:T(4,128)} %add.100) | data formatting | bytes 8388608 | tf_op jit(solution)/shard_map/add | solution.py:79
  58.8 76.4 %all-gather.6.cloned.1.call-done = bf16[256,4,2048]{2,1,0:T(4,128)(2,1)} async-done(((bf16[1,4,2048]{2,1,0:T(4,128)(2,1)}), bf16[256,4,2048]{2,1,0:T(4,128)(2,1)}) %all-gather.6.cloned.1.call-update) | async-done | bytes 4194320 | tf_op jit(solution)/shard_map/all_gather | solution.py:13
  135.3 6.9 %reshape.196 = bf16[1024,2048]{1,0:T(8,128)(2,1)} reshape(bf16[256,4,2048]{2,1,0:T(4,128)(2,1)} %all-gather.6.cloned.1.call-done) | data formatting | bytes 8388608
  142.2 111.8 %all-gather.4.cloned.1.call-done = bf16[2048,2048]{1,0:T(8,128)(2,1)} async-done(((bf16[8,2048]{1,0:T(8,128)(2,1)}), bf16[2048,2048]{1,0:T(8,128)(2,1)}) %all-gather.4.cloned.1.call-update) | async-done | bytes 8388624 | tf_op jit(solution)/shard_map/all_gather | solution.py:20
  254.1 19.9 %maximum_convert_fusion = bf16[1024,2048]{1,0:T(8,128)(2,1)} fusion(bf16[2048,2048]{1,0:T(8,128)(2,1)} %all-gather.4.cloned.1.call-done, bf16[1024,2048]{1,0:T(8,128)(2,1)} %reshape.196, f32[2048]{0:T(1024)S(1)} %copy-done.9, f32[2048]{0:T(1024)S(1)} %copy-done.10, f32[1024,1024]{1,0:T(8,128)} %add.101, bf16[1024,1024]{1,0:T(8,128)(2,1)S(1)} %bitcast.51), kind=kOutput, calls=%fused_computation.2 | convolution fusion | flops 12900630528 | bytes 23085056 | tf_op jit(solution)/shard_map/dot_general | solution.py:18
  274.0 3.4 %fusion.8 = bf16[1024,8]{0,1:T(8,128)(2,1)S(1)} fusion(bf16[1024,2048]{1,0:T(8,128)(2,1)} %maximum_convert_fusion, bf16[2048,8]{0,1:T(8,128)(2,1)S(1)} %copy-done.3, f32[8]{0:T(128)S(1)} %copy-done.7), kind=kOutput, calls=%fused_computation.13 | convolution fusion | flops 33570816 | bytes 4243488 | tf_op jit(solution)/shard_map/dot_general | solution.py:24
  277.4 0.2 copy.57
  277.6 0.3 convert_element_type.114
  277.8 0.5 broadcast.151
  278.3 0.7 reduce.12
  279.1 0.6 reshape.212
  279.7 5.8 %all-to-all-start.2 = ((bf16[32,2,128]{2,1,0:T(2,128)(2,1)}), bf16[32,2,128]{2,1,0:T(2,128)(2,1)S(1)}, u32[]{:S(2)}, u32[]{:S(2)}) async-start(bf16[32,2,128]{2,1,0:T(2,128)(2,1)} %reshape.212), calls=%async_computation.2 | async-start | bytes 32768 | tf_op jit(solution)/shard_map/all_to_all | solution.py:84
  285.5 0.1 max.35
  285.6 6.8 %all-to-all-done.2 = bf16[32,2,128]{2,1,0:T(2,128)(2,1)S(1)} async-done(((bf16[32,2,128]{2,1,0:T(2,128)(2,1)}), bf16[32,2,128]{2,1,0:T(2,128)(2,1)S(1)}, u32[]{:S(2)}, u32[]{:S(2)}) %all-to-all-start.2) | async-done | bytes 16416 | tf_op jit(solution)/shard_map/all_to_all | solution.py:84
  292.4 0.1 convert_reduce_fusion
  292.5 0.1 reshape.178
  292.6 0.7 gather_fusion.1
  293.3 0.1 fusion.14
  293.4 0.1 multiply_reduce_fusion
  293.6 0.6 select_reduce_fusion.1
  294.2 0.7 bitcast_multiply_fusion
  (41 shorter events, 0.4 us)
Async XLA Ops:
  7.2 41.9 %copy-start = (bf16[256,1024]{1,0:T(8,128)(2,1)S(1)}, bf16[256,1024]{1,0:T(8,128)(2,1)}, u32[]{:S(2)}) copy-start(bf16[256,1024]{1,0:T(8,128)(2,1)} %param.17) | copy-start | bytes 1572868
  7.2 128.1 %all-gather.6.cloned.1.call-start = ((), (), s32[]{:S(2)}) async-start(), calls=%async_computation.4 | async-start | bytes 4210688 | tf_op jit(solution)/shard_map/all_gather | solution.py:13
  7.9 246.1 %all-gather.4.cloned.1.call-start = ((), (), s32[]{:S(2)}) async-start(), calls=%async_computation.3 | async-start | bytes 8421376 | tf_op jit(solution)/shard_map/all_gather | solution.py:20
  13.2 27.0 %all-to-all-start.1 = ((s32[32,1,8]{2,1,0:T(1,128)}), s32[32,1,8]{2,1,0:T(1,128)S(1)}, u32[]{:S(2)}, u32[]{:S(2)}) async-start(s32[32,1,8]{2,1,0:T(1,128)} %bitcast.4), calls=%async_computation.1 | async-start | bytes 32768 | tf_op jit(solution)/shard_map/all_to_all | solution.py:76
  21.8 8.5 %copy-start.6 = (s32[192,4]{0,1:T(4,128)S(1)}, s32[192,4]{0,1:T(4,128)}, u32[]{:S(2)}) copy-start(s32[192,4]{0,1:T(4,128)} %param.25) | copy-start | bytes 9220
  21.8 8.8 %copy-start.2 = (bf16[128,1024]{1,0:T(8,128)(2,1)S(1)}, bf16[128,1024]{1,0:T(8,128)(2,1)}, u32[]{:S(2)}) copy-start(bf16[128,1024]{1,0:T(8,128)(2,1)} %param.16) | copy-start | bytes 786436
  37.5 10.0 %copy-start.4 = (s32[192,1]{0,1:T(1,128)S(1)}, s32[192,1]{0,1:T(1,128)}, u32[]{:S(2)}) copy-start(s32[192,1]{0,1:T(1,128)} %param.26) | copy-start | bytes 2308
  37.6 10.1 %copy-start.5 = (s32[192]{0:T(256)S(1)}, s32[192]{0:T(256)}, u32[]{:S(2)}) copy-start(s32[192]{0:T(256)} %param.24) | copy-start | bytes 2308
  40.2 102.0 %all-to-all-start = ((bf16[32,32,1024]{2,1,0:T(8,128)(2,1)}), bf16[32,32,1024]{2,1,0:T(8,128)(2,1)S(1)}, u32[]{:S(2)}, u32[]{:S(2)}) async-start(bf16[32,32,1024]{2,1,0:T(8,128)(2,1)} %reshape.173), calls=%async_computation | async-start | bytes 4194304 | tf_op jit(solution)/shard_map/all_to_all | solution.py:75
  58.8 195.2 %copy-start.9 = (f32[2048]{0:T(1024)S(1)}, f32[2048]{0:T(1024)}, u32[]{:S(2)}) copy-start(f32[2048]{0:T(1024)} %param.21) | copy-start | bytes 24580
  58.8 195.2 %copy-start.10 = (f32[2048]{0:T(1024)S(1)}, f32[2048]{0:T(1024)}, u32[]{:S(2)}) copy-start(f32[2048]{0:T(1024)} %param.19) | copy-start | bytes 24580
  254.1 19.9 %copy-start.3 = (bf16[2048,8]{0,1:T(8,128)(2,1)S(1)}, bf16[2048,8]{0,1:T(8,128)(2,1)}, u32[]{:S(2)}) copy-start(bf16[2048,8]{0,1:T(8,128)(2,1)} %param.22) | copy-start | bytes 98308
  254.1 19.9 %copy-start.7 = (f32[8]{0:T(128)S(1)}, f32[8]{0:T(128)}, u32[]{:S(2)}) copy-start(f32[8]{0:T(128)} %param.23) | copy-start | bytes 100
  274.0 19.3 %copy-start.1 = (s32[192,32]{0,1:T(8,128)S(1)}, s32[192,32]{0,1:T(8,128)}, u32[]{:S(2)}) copy-start(s32[192,32]{0,1:T(8,128)} %param.28) | copy-start | bytes 73732
  274.0 19.6 %copy-start.8 = (s32[192]{0:T(256)S(1)}, s32[192]{0:T(256)}, u32[]{:S(2)}) copy-start(s32[192]{0:T(256)} %param.29) | copy-start | bytes 2308
  279.7 12.7 %all-to-all-start.2 = ((bf16[32,2,128]{2,1,0:T(2,128)(2,1)}), bf16[32,2,128]{2,1,0:T(2,128)(2,1)S(1)}, u32[]{:S(2)}, u32[]{:S(2)}) async-start(bf16[32,2,128]{2,1,0:T(2,128)(2,1)} %reshape.212), calls=%async_computation.2 | async-start | bytes 32768 | tf_op jit(solution)/shard_map/all_to_all | solution.py:84
Sparse Core Ops, SparseCore 0:
  11.6 123.6 all-gather.5
  138.9 115.1 all-gather.3
where the time goes:
time: 302 us
  waiting for transfers between devices  196 us (65%)
  local copies, waits for them, and re-layouts  34.3 us (11%)
  matrix products  28 us (9%)
  starting transfers between devices  21.8 us (7%)
  between operations  14.3 us (5%)
  other arithmetic  6.85 us (2%)
    all_gather x1, waiting for transfers between devices, network(): lax.all_gather(w_second, ('trav', 'bulk'), axis=0, tiled=True)  112 us
    all_gather x1, waiting for transfers between devices, network(): lax.all_gather(w_first, ('trav', 'bulk'), axis=0, tiled=True)  76.4 us
    dot_general x1, matrix products, network(): jnp.dot(columns, lax.all_gather(w_second, ('trav', 'bulk'), axis=0, tiled...  19.9 us
    all_to_all x1, starting transfers between devices, body(): lax.all_to_all(slot_bucket, 'bulk', split_axis=0, concat_axis=0, tiled=True)  8.58 us
    add x2, local copies, waits for them, and re-layouts, body(): arrived_rows.reshape(slot_total, branch_slots, feature_count)  8.44 us
    unnamed x26, local copies, waits for them, and re-layouts  7.71 us
    all_to_all x1, starting transfers between devices, body(): lax.all_to_all(outgoing, 'bulk', split_axis=0, concat_axis=0, tiled=True)  7.38 us
    all_to_all x1, waiting for transfers between devices, body(): lax.all_to_all(evaluated.reshape(bulk_count, capacity * branch_slots * ac...  6.79 us
  transfers between devices with their start and end apart: 5, of which 3 were waited for; matrix products, arithmetic and copies ran while one was open for 13% of the time, Pallas kernels for 0%

commit v1 on v0

v1 whole, which is shorter than its diff:
```python
import functools

import jax
import jax.numpy as jnp
from jax import lax
from jax.experimental import pallas as pl
from jax.experimental.pallas import tpu as pltpu
from jax.sharding import PartitionSpec as P

MESH = pl.DeviceIdType.MESH
NZ, NY, NX, NC = 8, 4, 4, 2
NB = NY * NX * NC
TREMBLE = 0.05
PAR, KMAX, ACTIONS, F, H, CAP, VOCAB, BUCK, ANC = 192, 4, 8, 1024, 2048, 8, 128, 256, 48
HALF = H // 2
ROWS = PAR * KMAX
STAGES = (
    (0, 0, 384, 384, 256),
    (1, 0, 128, 256, 128),
    (1, 512, 256, 128, 128),
)
COPIES = 256
bf16, f32 = jnp.bfloat16, jnp.float32


def kernel(
    parents, act, table, w1, b1, w2, b2, wht, bh, counts, acts, owner, brow, legal, anc,
    out, outa,
    w1b, w2b, w1x, xs, h1, ss, gmat, ids_s, ids_r, rows_s, rows_r, pa, pt, pr,
    ssem, rsem, isem, irsem, gsem, grsem, lsem,
):
    z = lax.axis_index("trav")
    b = lax.axis_index("bulk")
    core = lax.rem(b, 2)
    x = lax.rem(lax.div(b, 2), NX)
    y = lax.div(b, 2 * NX)
    sibling = (z, b + 1 - 2 * core)
    other = 1 - core

    def dev(zz, yy, xx):
        return (lax.rem(zz + NZ, NZ), (lax.rem(yy + NY, NY) * NX + lax.rem(xx + NX, NX)) * 2 + core)

    barrier = pltpu.get_barrier_semaphore()

    def greet(j, _):
        pl.semaphore_signal(barrier, inc=1, device_id=(z, lax.rem(b + j, NB)), device_id_type=MESH)
        return 0

    lax.fori_loop(1, NB, greet, 0)
    for dz in (1, -1):
        pl.semaphore_signal(barrier, inc=1, device_id=dev(z + dz, y, x), device_id_type=MESH)

    ss[...] = jnp.full(ss.shape, -1.0, f32)
    ss[0:4, 0:PAR] = acts[...].astype(f32)
    ss[4:5, 0:PAR] = owner[...].astype(f32)
    ss[5:6, 0:PAR] = brow[...].astype(f32)
    st = ss[...].T
    lanes = lax.broadcasted_iota(jnp.int32, (256, 128), 1).astype(f32)
    sub2 = lax.broadcasted_iota(jnp.int32, (256, 256), 0).astype(f32)
    lane2 = lax.broadcasted_iota(jnp.int32, (256, 256), 1).astype(f32)
    owner_col = st[:, 4:5]
    hits = jnp.where(owner_col == lanes, 1.0, 0.0)
    below = jnp.where(sub2 > lane2, 1.0, 0.0).astype(bf16)
    rank = jnp.dot(below, hits.astype(bf16), preferred_element_type=f32)
    slot_col = owner_col * CAP + jnp.sum(rank * hits, axis=1, keepdims=True)
    gmat[...] = jnp.where(slot_col == lane2, 1.0, 0.0).astype(bf16)[0:PAR]
    owner_row = ss[4:5, :]
    hits_t = jnp.where(owner_row == sub2[0:NB], 1.0, 0.0)
    above = jnp.where(sub2 < lane2, 1.0, 0.0).astype(bf16)
    rank_t = jnp.dot(hits_t.astype(bf16), above, preferred_element_type=f32)
    slot_row = owner_row * CAP + jnp.sum(rank_t * hits_t, axis=0, keepdims=True)
    place_t = jnp.where(slot_row == sub2, 1.0, 0.0).astype(bf16)
    row_cols = jnp.broadcast_to(st[:, 5:6], (256, 128)).astype(bf16)
    ids_s[...] = jnp.dot(place_t, row_cols, preferred_element_type=f32)

    pl.semaphore_wait(barrier, NB - 1 + 2)

    counter = [0]
    started = []

    def send(src, dst, target):
        k = counter[0]
        counter[0] += 1
        copy = pltpu.make_async_remote_copy(
            src_ref=src, dst_ref=dst, send_sem=ssem.at[k], recv_sem=rsem.at[k],
            device_id=target, device_id_type=MESH,
        )
        copy.start()
        started.append(copy)
        return copy

    mine = pl.multiple_of(core * HALF, HALF)
    theirs = pl.multiple_of(other * HALF, HALF)
    to_sib = [
        send(w1.at[:, pl.ds(theirs, HALF)], w1x, sibling),
        send(w2.at[:, pl.ds(theirs, HALF)], w2b.at[z, y, x, pl.ds(pl.multiple_of(core * 8, 8), 8), :], sibling),
    ]
    own_w2 = pltpu.make_async_copy(
        w2.at[:, pl.ds(mine, HALF)], w2b.at[z, y, x, pl.ds(pl.multiple_of(core * 8, 8), 8), :], lsem.at[0]
    )
    own_w2.start()

    def eight(ref, i):
        return ref.at[pl.ds(pl.multiple_of(i * CAP, CAP), CAP), :]

    def id_copy(j):
        peer = lax.rem(b + j, NB)
        return pltpu.make_async_remote_copy(
            src_ref=eight(ids_s, peer), dst_ref=eight(ids_r, b), send_sem=isem.at[j], recv_sem=irsem.at[j],
            device_id=(z, peer), device_id_type=MESH,
        )

    def row_copy(j):
        peer = lax.rem(b + j, NB)
        return pltpu.make_async_remote_copy(
            src_ref=eight(rows_s, peer), dst_ref=eight(rows_r, b), send_sem=gsem.at[j], recv_sem=grsem.at[j],
            device_id=(z, peer), device_id_type=MESH,
        )

    def each_peer(action):
        def step(j, _):
            action(j)
            return 0

        lax.fori_loop(1, NB, step, 0)

    each_peer(lambda j: id_copy(j).start())
    own_ids = pltpu.make_async_copy(eight(ids_s, b), eight(ids_r, b), lsem.at[1])
    own_ids.start()

    to_sib[0].wait_recv()
    w1_own = w1[:, pl.ds(mine, HALF)]
    w1_sib = w1x[...]
    first = jnp.where(core == 0, w1_own.astype(f32), w1_sib.astype(f32))
    second = jnp.where(core == 0, w1_sib.astype(f32), w1_own.astype(f32))
    w1b[z, y, x] = jnp.concatenate([first, second], axis=0).astype(bf16)
    to_sib[1].wait_recv()
    own_w2.wait()

    class Stage:
        def __init__(self, layer, col, wa, wb, wc):
            self.buf = w1b if layer == 0 else w2b
            self.cols = {"A": (col, wa), "B": (col + wa, wb), "C": (col + wa + wb, wc)}
            self.done = 0
            self.flight = []

        def at(self, part, zs, ys, xs_):
            c0, w = self.cols[part]
            return self.buf.at[zs, ys, xs_, :, pl.ds(c0, w)]

        def block(self, part, axis, index, half=None):
            one = pl.ds(index, 1)
            if axis == "z" and part == "A":
                ys = pl.ds(0, NY) if half is None else pl.ds(half * NY // 2, NY // 2)
                return self.at(part, one, ys, pl.ds(x, 1))
            if axis == "z" and part == "B":
                xr = pl.ds(0, NX) if half is None else pl.ds(half * NX // 2, NX // 2)
                return self.at(part, one, pl.ds(y, 1), xr)
            if axis == "y" and part == "C":
                xr = pl.ds(0, NX) if half is None else pl.ds(half * NX // 2, NX // 2)
                return self.at(part, pl.ds(z, 1), one, xr)
            if axis == "z" and part == "C":
                ys = pl.ds(0, NY) if half is None else pl.ds(half * NY // 2, NY // 2)
                return self.at(part, one, ys, pl.ds(0, NX))
            zs = pl.ds(0, NZ) if half is None else pl.ds(half * NZ // 2, NZ // 2)
            if axis == "x":
                return self.at(part, zs, pl.ds(0, NY), one)
            return self.at(part, zs, one, pl.ds(0, NX))

        def ring(self, part, axis, d):
            n = {"z": NZ, "y": NY, "x": NX}[axis]
            me = {"z": z, "y": y, "x": x}[axis]
            for k, sign in enumerate((1, -1)):
                half = k if d == n // 2 - 1 else None
                src = self.block(part, axis, lax.rem(me - sign * d + n, n), half)
                target = dev(
                    z + sign * (axis == "z"), y + sign * (axis == "y"), x + sign * (axis == "x")
                )
                self.flight.append(send(src, src, target))

        def wait(self):
            for copy in self.flight:
                copy.wait_recv()
            self.flight = []

        def step(self):
            k = self.done
            self.done += 1
            self.wait()
            if k == 0:
                ca, wa = self.cols["A"]
                cb, wb = self.cols["B"]
                wc = self.cols["C"][1]
                own = self.buf.at[z, y, x]
                for d in (1, 3, 2):
                    ref = own.at[:, pl.ds(ca, wa)]
                    self.flight.append(send(ref, ref, dev(z, y + d, x)))
                    ref = own.at[:, pl.ds(cb, wb + wc)]
                    self.flight.append(send(ref, ref, dev(z, y, x + d)))
            elif k < 7:
                for part, axis, d in (
                    ("A", "z", k - 1) if k < 5 else ("A", "x", k - 5),
                    ("B", "z", k - 1) if k < 5 else ("B", "y", k - 5),
                    ("C", "y", k - 1) if k < 3 else ("C", "z", k - 3),
                ):
                    self.ring(part, axis, d)

    stages = [Stage(*s) for s in STAGES]
    for s in stages:
        s.step()
    s0, s1, s2 = stages
    s0.step()

    own_ids.wait()
    each_peer(lambda j: id_copy(j).wait_recv())
    ids = ids_r[...]
    onehot = jnp.concatenate(
        [jnp.where(ids == lanes, 1.0, 0.0).astype(bf16), jnp.where(ids == lanes + 128.0, 1.0, 0.0).astype(bf16)], axis=1
    )
    rows_s[...] = jnp.dot(onehot, table[...], preferred_element_type=f32).astype(bf16)
    s0.step()
    each_peer(lambda j: row_copy(j).start())
    own_rows = pltpu.make_async_copy(eight(rows_s, b), eight(rows_r, b), lsem.at[2])
    own_rows.start()

    s1.step()
    s0.step()
    act_rows = []
    for c in range(KMAX):
        oh = jnp.where(st[0:PAR, c : c + 1] == lanes[0:PAR], 1.0, 0.0).astype(bf16)
        rows = jnp.dot(oh, act[...], preferred_element_type=f32)
        xs[core, c * PAR : (c + 1) * PAR, :] = (parents[...].astype(f32) + rows).astype(bf16)
    s0.step()
    s1.step()
    own_rows.wait()
    each_peer(lambda j: row_copy(j).wait_recv())
    placed = jnp.dot(gmat[...], rows_r[...], preferred_element_type=f32)
    for c in range(KMAX):
        base = xs[core, c * PAR : (c + 1) * PAR, :].astype(f32)
        xs[core, c * PAR : (c + 1) * PAR, :] = (base + placed).astype(bf16)
    x_copy = send(xs.at[core], xs.at[core], sibling)

    for s in (s2, s0, s1, s2, s0, s1, s0, s2, s1):
        s.step()

    RC = ROWS // 2
    w1f = w1b.reshape(F, HALF)
    w2f = w2b.reshape(H, HALF)

    def layer_one(o, r):
        def tile(n, _):
            c0 = pl.multiple_of(n * 256, 256)
            acc = jnp.dot(xs[o, r * RC : (r + 1) * RC, :], w1f[:, pl.ds(c0, 256)], preferred_element_type=f32)
            bias = b1[:, pl.ds(pl.multiple_of(mine + c0, 256), 256)]
            h1[core, o, r * RC : (r + 1) * RC, pl.ds(c0, 256)] = jnp.maximum(acc + bias, 0.0).astype(bf16)
            return 0

        lax.fori_loop(0, HALF // 256, tile, 0)
        part = h1.at[core, o, pl.ds(r * RC, RC), :]
        return send(part, part, sibling)

    h_copies = [layer_one(core, 0), layer_one(core, 1)]
    s2.step()
    s1.step()
    x_copy.wait_recv()
    h_copies += [layer_one(other, 0), layer_one(other, 1)]
    s2.step()
    s1.step()
    for copy in h_copies:
        copy.wait_recv()

    def layer_two(o, r, col0, tiles):
        def tile(n, total):
            c0 = pl.multiple_of(col0 + n * 256, 256)
            acc = jnp.dot(h1[0, o, r * RC : (r + 1) * RC, :], w2f[0:HALF, pl.ds(c0, 256)], preferred_element_type=f32)
            acc += jnp.dot(h1[1, o, r * RC : (r + 1) * RC, :], w2f[HALF:H, pl.ds(c0, 256)], preferred_element_type=f32)
            g0 = pl.multiple_of(mine + c0, 256)
            hid = jnp.maximum(acc + b2[:, pl.ds(g0, 256)], 0.0).astype(bf16)
            return total + lax.dot_general(
                hid, wht[:, pl.ds(g0, 256)], (((1,), (1,)), ((), ())), preferred_element_type=f32
            )

        return lax.fori_loop(0, tiles, tile, jnp.zeros((RC, ACTIONS), f32))

    share = jnp.where(core == 0, 1.0, 0.0)
    for i, (o, r) in enumerate(((other, 0), (other, 1), (core, 0), (core, 1))):
        pa[o, r * RC : (r + 1) * RC, :] = layer_two(o, r, 0, 2) + bh[...] * share
        if i == 1:
            s2.step()
    s2.step()

    def finish(o, r):
        total = pa[o, r * RC : (r + 1) * RC, :] + layer_two(o, r, 512, 2)
        for i in range(2):
            pt[o, r * 2 + i] = total[i * PAR : (i + 1) * PAR, :].T

    finish(other, 0)
    finish(other, 1)
    p_copy = send(pt.at[other], pr, sibling)
    finish(core, 0)
    finish(core, 1)
    p_copy.wait_recv()

    count = counts[...]
    first_action = jnp.where(lax.broadcasted_iota(jnp.int32, (ACTIONS, PAR), 0) == 0, 1.0, 0.0)
    value = jnp.zeros((1, PAR), f32)
    for c in range(KMAX):
        adv = pt[core, c] + pr[c]
        allowed = jnp.maximum(legal[c * ACTIONS : (c + 1) * ACTIONS, :].astype(f32), first_action)
        positive = allowed * (jnp.maximum(adv, 0.0) + TREMBLE)
        sigma = positive / jnp.sum(positive, axis=0, keepdims=True)
        live = jnp.where(count > c, 1.0, 0.0)
        out[c * ACTIONS : (c + 1) * ACTIONS, :] = sigma * live
        value += live * jnp.sum(sigma * adv, axis=0, keepdims=True)
    value = value / count.astype(f32)
    nodes = lax.broadcasted_iota(jnp.int32, (ANC, PAR), 0)
    sums = jnp.sum(jnp.where(nodes == anc[...], value, 0.0), axis=1, keepdims=True)
    diag = lax.broadcasted_iota(jnp.int32, (ANC, ANC), 0) == lax.broadcasted_iota(jnp.int32, (ANC, ANC), 1)
    outa[...] = jnp.sum(jnp.where(diag, sums, 0.0), axis=0, keepdims=True)

    for copy in started:
        copy.wait_send()
    each_peer(lambda j: id_copy(j).wait_send())
    each_peer(lambda j: row_copy(j).wait_send())


def body(
    parents, act_table, bucket_table, w_first, b_first, w_second, b_second, w_head, b_head,
    branch_counts, sampled_actions, bucket_owner, bucket_row, legal_mask, ancestor,
):
    row = lambda a: a.reshape(1, a.shape[0])
    vmem = pl.BlockSpec(memory_space=pltpu.VMEM)
    dma = pltpu.SemaphoreType.DMA
    out, outa = pl.pallas_call(
        kernel,
        out_shape=(jax.ShapeDtypeStruct((KMAX * ACTIONS, PAR), f32), jax.ShapeDtypeStruct((1, ANC), f32)),
        in_specs=[vmem] * 15,
        out_specs=(vmem, vmem),
        scratch_shapes=[
            pltpu.VMEM((NZ, NY, NX, 8, HALF), bf16),
            pltpu.VMEM((NZ, NY, NX, 16, HALF), bf16),
            pltpu.VMEM((4, HALF), bf16),
            pltpu.VMEM((2, ROWS, F), bf16),
            pltpu.VMEM((2, 2, ROWS, HALF), bf16),
            pltpu.VMEM((128, 256), f32),
            pltpu.VMEM((PAR, 256), bf16),
            pltpu.VMEM((256, 128), f32),
            pltpu.VMEM((256, 128), f32),
            pltpu.VMEM((256, F), bf16),
            pltpu.VMEM((256, F), bf16),
            pltpu.VMEM((2, ROWS, ACTIONS), f32),
            pltpu.VMEM((2, KMAX, ACTIONS, PAR), f32),
            pltpu.VMEM((KMAX, ACTIONS, PAR), f32),
            dma((COPIES,)),
            dma((COPIES,)),
            dma((NB,)),
            dma((NB,)),
            dma((NB,)),
            dma((NB,)),
            dma((4,)),
        ],
        compiler_params=pltpu.CompilerParams(
            collective_id=0, has_side_effects=True, vmem_limit_bytes=56 * 1024 * 1024
        ),
    )(
        parents, act_table, bucket_table, w_first, row(b_first), w_second, row(b_second), w_head.T, row(b_head),
        row(branch_counts), sampled_actions.T, bucket_owner.T, row(bucket_row), legal_mask.T, row(ancestor),
    )
    return out.T, outa.reshape(ANC)


def solution(mesh):
    rows = P(("trav", "bulk"), None)
    flat = P(("trav", "bulk"))
    return jax.shard_map(
        body,
        mesh=mesh,
        in_specs=(rows, P(), P("bulk", None), rows, P(), rows, P(), P(), P(), flat, rows, rows, flat, rows, flat),
        out_specs=(rows, flat),
        check_vma=False,
    )
```

time: 302 us -> 84.3 us (0.28)
  waiting for transfers between devices: 196 us -> 0 us
  Pallas kernels: 0 us -> 81.5 us
  local copies, waits for them, and re-layouts: 34.3 us -> 1.89 us
  matrix products: 28 us -> 0 us
  starting transfers between devices: 21.8 us -> 0 us
  between operations: 14.3 us -> 0.65 us
  other arithmetic: 6.85 us -> 0 us
    all_gather x2 -> x0, waiting for transfers between devices: 188 us -> none  [the longest x1 112 us: network(): lax.all_gather(w_second, ('trav', 'bulk'), axis=0, tiled=True)]
    pallas_call x0 -> x1, Pallas kernels: none -> 81.5 us  [body(): pl.pallas_call(kernel, out_shape=(jax.ShapeDtypeStruct((KMAX * ACTIONS, P...]
    dot_general x4 -> x0, matrix products: 28 us -> none  [the longest x1 19.9 us: network(): jnp.dot(columns, lax.all_gather(w_second, ('trav', 'bulk'), axis=0, tiled...]
    all_to_all x3 -> x0, starting transfers between devices: 21.7 us -> none  [the longest x1 8.58 us: body(): lax.all_to_all(slot_bucket, 'bulk', split_axis=0, concat_axis=0, tiled=True)]
    reshape x5 -> x0, local copies, waits for them, and re-layouts: 10 us -> none  [the longest x1 4.97 us: body(): jnp.repeat(parents.astype(jnp.float32), branch_slots, axis=0) + act_rows]
    add x2 -> x0, local copies, waits for them, and re-layouts: 8.44 us -> none  [body(): arrived_rows.reshape(slot_total, branch_slots, feature_count)]
    all_to_all x3 -> x0, waiting for transfers between devices: 6.79 us -> none  [the longest x1 6.79 us: body(): lax.all_to_all(evaluated.reshape(bulk_count, capacity * branch_slots * ac...]
    unnamed x26 -> x4, local copies, waits for them, and re-layouts: 7.71 us -> 1.89 us
  transfers between devices with their start and end apart: 5 -> 0, of which waited for: 3 -> 0; matrix products, arithmetic and copies ran while one was open for 13% -> 0% of each run, Pallas kernels for 0% -> 0%
where the time goes in v1:
time: 84.3 us; the launch traced here: 84.1 us
  Pallas kernels  81.5 us (97%)
  local copies, waits for them, and re-layouts  1.89 us (2%)
    pallas_call x1, Pallas kernels, body(): pl.pallas_call(kernel, out_shape=(jax.ShapeDtypeStruct((KMAX * ACTIONS, P...  81.5 us
    unnamed x4, local copies, waits for them, and re-layouts  1.89 us

profile of v1, /device:TPU:1, one launch (start us, length us, event | category | flops | bytes accessed | tf_op | source)
XLA Modules:
  0.0 84.1 jit_solution(14954608362365110645)
XLA Ops:
  0.6 81.5 %shard_map.158 = (f32[32,192]{1,0:T(8,128)}, f32[1,48]{1,0:T(1,128)}) custom-call(bf16[192,1024]{1,0:T(8,128)(2,1)} %parents.1, bf16[128,1024]{1,0:T(8,128)(2,1)} %act.1, bf16[256,1024]{1,0:T(8,128)(2,1)} %table.1, bf16[4,2048]{1,0:T(4,128)(2,1)} %w1.1, f32[1,2048]{1,0:T(1,128)} %bitcast.15, bf16[8,2048]{1,0:T(8,128)(2,1)} %w2.1, f32[1,2048]{1,0:T(1,128)} %bitcast.16, ...), custom_call_target="tpu_custom_call" | custom-call | tf_op jit(solution)/shard_map/pallas_call | solution.py:334
  82.2 0.0 copy-start
  82.2 1.4 %copy.19 = f32[192,32]{0,1:T(8,128)} copy(f32[192,32]{0,1:T(8,128)} %bitcast.14) | data formatting | bytes 49152
  83.6 0.0 copy-done
  83.6 0.5 copy.20
Async XLA Ops:
  82.2 1.4 %copy-start = (f32[1,48]{1,0:T(1,128)S(1)}, f32[1,48]{1,0:T(1,128)}, u32[]{:S(2)}) copy-start(f32[1,48]{1,0:T(1,128)} %get-tuple-element.5) | copy-start | bytes 580

commit v2 on v1

v2 whole, which is shorter than its diff:
```python
import functools

import jax
import jax.numpy as jnp
from jax import lax
from jax.experimental import pallas as pl
from jax.experimental.pallas import tpu as pltpu
from jax.sharding import PartitionSpec as P

MESH = pl.DeviceIdType.MESH
NZ, NY, NX, NC = 8, 4, 4, 2
NB = NY * NX * NC
TREMBLE = 0.05
PAR, KMAX, ACTIONS, F, H, CAP, VOCAB, BUCK, ANC = 192, 4, 8, 1024, 2048, 8, 128, 256, 48
HALF = H // 2
ROWS = PAR * KMAX
STAGES = (
    (0, 0, 384, 384, 256),
    (1, 0, 128, 128, 256),
    (1, 512, 128, 128, 256),
)
COPIES = 256
INPUTS = (
    "parents", "act", "table", "w1", "b1", "w2", "b2", "wht", "bh", "counts", "acts", "owner", "brow", "legal", "anc"
)
bf16, f32 = jnp.bfloat16, jnp.float32


def kernel(*refs):
    n_in = len(INPUTS)
    inputs, (out, outa), inside = refs[:n_in], refs[n_in : n_in + 2], refs[n_in + 2 : 2 * n_in + 2]
    body_of_kernel(inputs, inside, out, outa, *refs[2 * n_in + 2 :])


def body_of_kernel(
    inputs, inside, out, outa,
    w1b, w2b, w1x, xs, h1, ss, gmat, ids_s, ids_r, rows_s, rows_r, pa, pt, pr,
    ssem, rsem, isem, irsem, gsem, grsem, lsem, nsem,
):
    parents, act, table, w1, b1, w2, b2, wht, bh, counts, acts, owner, brow, legal, anc = inside
    loads = [pltpu.make_async_copy(src, dst, nsem.at[k]) for k, (src, dst) in enumerate(zip(inputs, inside))]
    by_name = dict(zip(INPUTS, loads))
    for name in ("w1", "w2", "acts", "owner", "brow"):
        by_name[name].start()
    z = lax.axis_index("trav")
    b = lax.axis_index("bulk")
    core = lax.rem(b, 2)
    x = lax.rem(lax.div(b, 2), NX)
    y = lax.div(b, 2 * NX)
    sibling = (z, b + 1 - 2 * core)
    other = 1 - core

    def dev(zz, yy, xx):
        return (lax.rem(zz + NZ, NZ), (lax.rem(yy + NY, NY) * NX + lax.rem(xx + NX, NX)) * 2 + core)

    barrier = pltpu.get_barrier_semaphore()

    def greet(j, _):
        pl.semaphore_signal(barrier, inc=1, device_id=(z, lax.rem(b + j, NB)), device_id_type=MESH)
        return 0

    lax.fori_loop(1, NB, greet, 0)
    for dz in range(1, NZ):
        pl.semaphore_signal(barrier, inc=1, device_id=dev(z + dz, y, x), device_id_type=MESH)

    rest = [n for n in INPUTS if n not in ("w1", "w2", "acts", "owner", "brow")]
    for name in rest:
        by_name[name].start()

    pl.semaphore_wait(barrier, NB - 1 + NZ - 1)

    counter = [0]
    started = []

    def send(src, dst, target):
        k = counter[0]
        counter[0] += 1
        copy = pltpu.make_async_remote_copy(
            src_ref=src, dst_ref=dst, send_sem=ssem.at[k], recv_sem=rsem.at[k],
            device_id=target, device_id_type=MESH,
        )
        copy.start()
        started.append(copy)
        return copy

    by_name["w1"].wait()
    by_name["w2"].wait()
    mine = pl.multiple_of(core * HALF, HALF)
    theirs = pl.multiple_of(other * HALF, HALF)
    to_sib = [
        send(w1.at[:, pl.ds(theirs, HALF)], w1x, sibling),
        send(w2.at[:, pl.ds(theirs, HALF)], w2b.at[z, y, x, pl.ds(pl.multiple_of(core * 8, 8), 8), :], sibling),
    ]
    own_w2 = pltpu.make_async_copy(
        w2.at[:, pl.ds(mine, HALF)], w2b.at[z, y, x, pl.ds(pl.multiple_of(core * 8, 8), 8), :], lsem.at[0]
    )
    own_w2.start()

    for name in ("acts", "owner", "brow"):
        by_name[name].wait()
    ss[...] = jnp.full(ss.shape, -1.0, f32)
    ss[0:4, 0:PAR] = acts[...].astype(f32)
    ss[4:5, 0:PAR] = owner[...].astype(f32)
    ss[5:6, 0:PAR] = brow[...].astype(f32)
    st = ss[...].T
    lanes = lax.broadcasted_iota(jnp.int32, (256, 128), 1).astype(f32)
    sub2 = lax.broadcasted_iota(jnp.int32, (256, 256), 0).astype(f32)
    lane2 = lax.broadcasted_iota(jnp.int32, (256, 256), 1).astype(f32)
    owner_col = st[:, 4:5]
    hits = jnp.where(owner_col == lanes, 1.0, 0.0)
    below = jnp.where(sub2 > lane2, 1.0, 0.0).astype(bf16)
    rank = jnp.dot(below, hits.astype(bf16), preferred_element_type=f32)
    slot_col = owner_col * CAP + jnp.sum(rank * hits, axis=1, keepdims=True)
    gmat[...] = jnp.where(slot_col == lane2, 1.0, 0.0).astype(bf16)[0:PAR]
    owner_row = ss[4:5, :]
    hits_t = jnp.where(owner_row == sub2[0:NB], 1.0, 0.0)
    above = jnp.where(sub2 < lane2, 1.0, 0.0).astype(bf16)
    rank_t = jnp.dot(hits_t.astype(bf16), above, preferred_element_type=f32)
    slot_row = owner_row * CAP + jnp.sum(rank_t * hits_t, axis=0, keepdims=True)
    place_t = jnp.where(slot_row == sub2, 1.0, 0.0).astype(bf16)
    row_cols = jnp.broadcast_to(st[:, 5:6], (256, 128)).astype(bf16)
    ids_s[...] = jnp.dot(place_t, row_cols, preferred_element_type=f32)

    def eight(ref, i):
        return ref.at[pl.ds(pl.multiple_of(i * CAP, CAP), CAP), :]

    def id_copy(j):
        peer = lax.rem(b + j, NB)
        return pltpu.make_async_remote_copy(
            src_ref=eight(ids_s, peer), dst_ref=eight(ids_r, b), send_sem=isem.at[j], recv_sem=irsem.at[j],
            device_id=(z, peer), device_id_type=MESH,
        )

    def row_copy(j):
        peer = lax.rem(b + j, NB)
        return pltpu.make_async_remote_copy(
            src_ref=eight(rows_s, peer), dst_ref=eight(rows_r, b), send_sem=gsem.at[j], recv_sem=grsem.at[j],
            device_id=(z, peer), device_id_type=MESH,
        )

    def each_peer(action):
        def step(j, _):
            action(j)
            return 0

        lax.fori_loop(1, NB, step, 0)

    each_peer(lambda j: id_copy(j).start())
    own_ids = pltpu.make_async_copy(eight(ids_s, b), eight(ids_r, b), lsem.at[1])
    own_ids.start()

    to_sib[0].wait_recv()
    w1_own = w1[:, pl.ds(mine, HALF)]
    w1_sib = w1x[...]
    first = jnp.where(core == 0, w1_own.astype(f32), w1_sib.astype(f32))
    second = jnp.where(core == 0, w1_sib.astype(f32), w1_own.astype(f32))
    w1b[z, y, x] = jnp.concatenate([first, second], axis=0).astype(bf16)
    to_sib[1].wait_recv()
    own_w2.wait()

    class Stage:
        def __init__(self, layer, col, wa, wb, wc):
            self.buf = w1b if layer == 0 else w2b
            self.cols = {"A": (col, wa), "B": (col + wa, wb), "C": (col + wa + wb, wc)}
            self.ab_done = self.c_done = 0
            self.flight = {"A": {}, "B": {}, "C": {}}
            self.late = {"A": [], "B": [], "C": []}

        def at(self, part, zs, ys, xs_):
            c0, w = self.cols[part]
            return self.buf.at[zs, ys, xs_, :, pl.ds(c0, w)]

        def block(self, part, index, half):
            one = pl.ds(index, 1)
            if part == "C":
                return self.at(part, one, pl.ds(half * NY // 2, NY // 2), pl.ds(0, NX))
            zs = pl.ds(half * NZ // 2, NZ // 2)
            if part == "A":
                return self.at(part, zs, pl.ds(0, NY), one)
            return self.at(part, zs, one, pl.ds(0, NX))

        def ring(self, part, d):
            n, me, axis = {"A": (NX, x, "x"), "B": (NY, y, "y"), "C": (NZ, z, "z")}[part]
            before = self.flight[part]
            self.flight[part] = {}
            for k, sign in enumerate((1, -1)):
                target = dev(z + sign * (axis == "z"), y + sign * (axis == "y"), x + sign * (axis == "x"))
                for half in (k, 1 - k) if d < n // 2 - 1 else (k,):
                    if d > 0:
                        before.pop((k, half)).wait_recv()
                    src = self.block(part, lax.rem(me - sign * d + n, n), half)
                    self.flight[part][k, half] = send(src, src, target)
            self.late[part].extend(before.values() if d > 0 else ())

        def direct(self, part, src, targets):
            for target in targets:
                self.flight[part][len(self.flight[part])] = send(src, src, target)

        def wait(self, part):
            for copy in [*self.flight[part].values(), *self.late[part]]:
                copy.wait_recv()
            self.flight[part], self.late[part] = {}, []

        def ab(self):
            k = self.ab_done
            self.ab_done += 1
            if k == 0:
                c0, c1 = self.cols["A"][0], self.cols["C"][0]
                own = self.buf.at[z, y, x, :, pl.ds(c0, c1 - c0)]
                self.direct("A", own, [dev(z + d, y, x) for d in (4, 3, 5, 2, 6, 1, 7)])
            elif k == 1:
                self.wait("A")
                every, one = pl.ds(0, NZ), pl.ds(y, 1)
                self.direct("A", self.at("A", every, one, pl.ds(x, 1)), [dev(z, y + d, x) for d in (2, 1, 3)])
                self.direct("B", self.at("B", every, one, pl.ds(x, 1)), [dev(z, y, x + d) for d in (2, 1, 3)])
            else:
                for part in "AB":
                    if k in (2, 4):
                        self.wait(part)
                    if k < 4:
                        self.ring(part, k - 2)

        def c(self):
            k = self.c_done
            self.c_done += 1
            if k == 0:
                c0, w = self.cols["C"]
                self.direct("C", self.buf.at[z, y, x, :, pl.ds(c0, w)], [dev(z, y, x + d) for d in (2, 1, 3)])
            elif k == 1:
                self.wait("C")
                block = self.at("C", pl.ds(z, 1), pl.ds(y, 1), pl.ds(0, NX))
                self.direct("C", block, [dev(z, y + d, x) for d in (2, 1, 3)])
            else:
                if k in (2, 6):
                    self.wait("C")
                if k < 6:
                    self.ring("C", k - 2)

    stages = [Stage(*s) for s in STAGES]
    s0, s1, s2 = stages

    s0.ab()
    s0.c()
    s1.c()
    s1.ab()
    s2.c()
    s2.ab()
    s0.c()
    s1.c()
    s2.c()

    for name in rest:
        by_name[name].wait()
    own_ids.wait()
    each_peer(lambda j: id_copy(j).wait_recv())
    ids = ids_r[...]
    onehot = jnp.concatenate(
        [jnp.where(ids == lanes, 1.0, 0.0).astype(bf16), jnp.where(ids == lanes + 128.0, 1.0, 0.0).astype(bf16)], axis=1
    )
    rows_s[...] = jnp.dot(onehot, table[...], preferred_element_type=f32).astype(bf16)
    each_peer(lambda j: row_copy(j).start())
    own_rows = pltpu.make_async_copy(eight(rows_s, b), eight(rows_r, b), lsem.at[2])
    own_rows.start()
    s0.c()
    s1.c()
    s0.ab()
    s1.ab()
    s2.ab()

    act_rows = []
    for c in range(KMAX):
        oh = jnp.where(st[0:PAR, c : c + 1] == lanes[0:PAR], 1.0, 0.0).astype(bf16)
        rows = jnp.dot(oh, act[...], preferred_element_type=f32)
        xs[core, c * PAR : (c + 1) * PAR, :] = (parents[...].astype(f32) + rows).astype(bf16)
    s0.c()
    s2.c()
    s1.c()
    s0.ab()
    s0.c()
    own_rows.wait()
    each_peer(lambda j: row_copy(j).wait_recv())
    placed = jnp.dot(gmat[...], rows_r[...], preferred_element_type=f32)
    for c in range(KMAX):
        base = xs[core, c * PAR : (c + 1) * PAR, :].astype(f32)
        xs[core, c * PAR : (c + 1) * PAR, :] = (base + placed).astype(bf16)
    x_copy = send(xs.at[core], xs.at[core], sibling)

    s2.c()
    s1.c()
    s0.c()
    s0.ab()
    s1.ab()
    s0.c()
    s0.ab()

    RC = ROWS // 2
    w1f = w1b.reshape(F, HALF)
    w2f = w2b.reshape(H, HALF)

    def layer_one(o, r):
        rows = slice(r * RC, (r + 1) * RC)
        for c0 in range(0, HALF, 512):
            acc = jnp.dot(xs[o, rows, :], w1f[:, c0 : c0 + 512], preferred_element_type=f32)
            bias = b1[:, pl.ds(pl.multiple_of(mine + c0, 512), 512)]
            h1[core, o, rows, c0 : c0 + 512] = jnp.maximum(acc + bias, 0.0).astype(bf16)
        part = h1.at[core, o, pl.ds(r * RC, RC), :]
        return send(part, part, sibling)

    h_copies = [layer_one(core, 0)]
    s2.c()
    s2.ab()
    s1.c()
    h_copies.append(layer_one(core, 1))
    s1.ab()
    x_copy.wait_recv()
    h_copies.append(layer_one(other, 0))
    s2.c()
    h_copies.append(layer_one(other, 1))
    s2.ab()
    s1.ab()
    s1.c()
    for copy in h_copies:
        copy.wait_recv()

    def layer_two(o, c0):
        acc = jnp.dot(h1[0, o], w2f[0:HALF, c0 : c0 + 512], preferred_element_type=f32)
        acc += jnp.dot(h1[1, o], w2f[HALF:H, c0 : c0 + 512], preferred_element_type=f32)
        g0 = pl.multiple_of(mine + c0, 512)
        hid = jnp.maximum(acc + b2[:, pl.ds(g0, 512)], 0.0).astype(bf16)
        return lax.dot_general(hid, wht[:, pl.ds(g0, 512)], (((1,), (1,)), ((), ())), preferred_element_type=f32)

    share = jnp.where(core == 0, 1.0, 0.0)
    for o in (other, core):
        pa[o] = layer_two(o, 0) + bh[...] * share
    s2.ab()
    s2.c()

    def finish(o):
        total = pa[o] + layer_two(o, 512)
        for c in range(KMAX):
            pt[o, c] = total[c * PAR : (c + 1) * PAR, :].T

    finish(other)
    p_copy = send(pt.at[other], pr, sibling)
    finish(core)
    p_copy.wait_recv()

    count = counts[...]
    first_action = jnp.where(lax.broadcasted_iota(jnp.int32, (ACTIONS, PAR), 0) == 0, 1.0, 0.0)
    value = jnp.zeros((1, PAR), f32)
    for c in range(KMAX):
        adv = pt[core, c] + pr[c]
        allowed = jnp.maximum(legal[c * ACTIONS : (c + 1) * ACTIONS, :].astype(f32), first_action)
        positive = allowed * (jnp.maximum(adv, 0.0) + TREMBLE)
        sigma = positive / jnp.sum(positive, axis=0, keepdims=True)
        live = jnp.where(count > c, 1.0, 0.0)
        out[c * ACTIONS : (c + 1) * ACTIONS, :] = sigma * live
        value += live * jnp.sum(sigma * adv, axis=0, keepdims=True)
    value = value / count.astype(f32)
    nodes = lax.broadcasted_iota(jnp.int32, (ANC, PAR), 0)
    sums = jnp.sum(jnp.where(nodes == anc[...], value, 0.0), axis=1, keepdims=True)
    diag = lax.broadcasted_iota(jnp.int32, (ANC, ANC), 0) == lax.broadcasted_iota(jnp.int32, (ANC, ANC), 1)
    outa[...] = jnp.sum(jnp.where(diag, sums, 0.0), axis=0, keepdims=True)

    for copy in started:
        copy.wait_send()
    each_peer(lambda j: id_copy(j).wait_send())
    each_peer(lambda j: row_copy(j).wait_send())


def body(
    parents, act_table, bucket_table, w_first, b_first, w_second, b_second, w_head, b_head,
    branch_counts, sampled_actions, bucket_owner, bucket_row, legal_mask, ancestor,
):
    row = lambda a: a.reshape(1, a.shape[0])
    vmem = pl.BlockSpec(memory_space=pltpu.VMEM)
    operands = (
        parents, act_table, bucket_table, w_first, row(b_first), w_second, row(b_second), w_head.T, row(b_head),
        row(branch_counts), sampled_actions.T, bucket_owner.T, row(bucket_row), legal_mask.T, row(ancestor),
    )
    dma = pltpu.SemaphoreType.DMA
    out, outa = pl.pallas_call(
        kernel,
        out_shape=(jax.ShapeDtypeStruct((KMAX * ACTIONS, PAR), f32), jax.ShapeDtypeStruct((1, ANC), f32)),
        in_specs=[pl.BlockSpec(memory_space=pl.ANY)] * len(operands),
        out_specs=(vmem, vmem),
        scratch_shapes=[pltpu.VMEM(a.shape, a.dtype) for a in operands] + [
            pltpu.VMEM((NZ, NY, NX, 8, HALF), bf16),
            pltpu.VMEM((NZ, NY, NX, 16, HALF), bf16),
            pltpu.VMEM((4, HALF), bf16),
            pltpu.VMEM((2, ROWS, F), bf16),
            pltpu.VMEM((2, 2, ROWS, HALF), bf16),
            pltpu.VMEM((128, 256), f32),
            pltpu.VMEM((PAR, 256), bf16),
            pltpu.VMEM((256, 128), f32),
            pltpu.VMEM((256, 128), f32),
            pltpu.VMEM((256, F), bf16),
            pltpu.VMEM((256, F), bf16),
            pltpu.VMEM((2, ROWS, ACTIONS), f32),
            pltpu.VMEM((2, KMAX, ACTIONS, PAR), f32),
            pltpu.VMEM((KMAX, ACTIONS, PAR), f32),
            dma((COPIES,)),
            dma((COPIES,)),
            dma((NB,)),
            dma((NB,)),
            dma((NB,)),
            dma((NB,)),
            dma((4,)),
            dma((len(operands),)),
        ],
        compiler_params=pltpu.CompilerParams(
            collective_id=0, has_side_effects=True, vmem_limit_bytes=56 * 1024 * 1024
        ),
    )(*operands)
    return out.T, outa.reshape(ANC)


def solution(mesh):
    rows = P(("trav", "bulk"), None)
    flat = P(("trav", "bulk"))
    return jax.shard_map(
        body,
        mesh=mesh,
        in_specs=(rows, P(), P("bulk", None), rows, P(), rows, P(), P(), P(), flat, rows, rows, flat, rows, flat),
        out_specs=(rows, flat),
        check_vma=False,
    )
```

time: 84.3 us -> 68 us (0.81)
  Pallas kernels: 81.5 us -> 65.3 us
    pallas_call x1, Pallas kernels: 81.5 us -> 65.3 us  [body(): pl.pallas_call(kernel, out_shape=(jax.ShapeDtypeStruct((KMAX * ACTIONS, P...]
where the time goes in v2:
time: 68 us; the launch traced here: 67.8 us
  Pallas kernels  65.3 us (96%)
  local copies, waits for them, and re-layouts  1.89 us (3%)
    pallas_call x1, Pallas kernels, body(): pl.pallas_call(kernel, out_shape=(jax.ShapeDtypeStruct((KMAX * ACTIONS, P...  65.3 us
    unnamed x4, local copies, waits for them, and re-layouts  1.89 us

profile of v2, /device:TPU:1, one launch (start us, length us, event | category | flops | bytes accessed | tf_op | source)
XLA Modules:
  0.0 67.8 jit_solution(1701038639644349845)
XLA Ops:
  0.6 65.3 %shard_map.158 = (f32[32,192]{1,0:T(8,128)}, f32[1,48]{1,0:T(1,128)}) custom-call(bf16[192,1024]{1,0:T(8,128)(2,1)} %refs_0_.1, bf16[128,1024]{1,0:T(8,128)(2,1)} %refs_1_.1, bf16[256,1024]{1,0:T(8,128)(2,1)} %refs_2_.1, bf16[4,2048]{1,0:T(4,128)(2,1)} %refs_3_.1, f32[1,2048]{1,0:T(1,128)} %bitcast.15, bf16[8,2048]{1,0:T(8,128)(2,1)} %refs_5_.1, ...), custom_call_target="tpu_custom_call" | custom-call | tf_op jit(solution)/shard_map/pallas_call | solution.py:382
  65.9 0.0 copy-start
  65.9 1.4 %copy.19 = f32[192,32]{0,1:T(8,128)} copy(f32[192,32]{0,1:T(8,128)} %bitcast.14) | data formatting | bytes 49152
  67.3 0.0 copy-done
  67.3 0.5 copy.20
Async XLA Ops:
  65.9 1.4 %copy-start = (f32[1,48]{1,0:T(1,128)S(1)}, f32[1,48]{1,0:T(1,128)}, u32[]{:S(2)}) copy-start(f32[1,48]{1,0:T(1,128)} %get-tuple-element.5) | copy-start | bytes 580

commit v3 on v2

--- a/solution.py
+++ b/solution.py
@@ -17,7 +17,7 @@
 STAGES = (
     (0, 0, 384, 384, 256),
     (1, 0, 128, 128, 256),
-    (1, 512, 128, 128, 256),
+    (1, 512, 256, 128, 128),
 )
 COPIES = 256
 INPUTS = (
@@ -163,6 +163,7 @@
             self.buf = w1b if layer == 0 else w2b
             self.cols = {"A": (col, wa), "B": (col + wa, wb), "C": (col + wa + wb, wc)}
             self.ab_done = self.c_done = 0
+            self.turned = layer == 1
             self.flight = {"A": {}, "B": {}, "C": {}}
             self.late = {"A": [], "B": [], "C": []}
 
@@ -225,11 +226,19 @@
             self.c_done += 1
             if k == 0:
                 c0, w = self.cols["C"]
-                self.direct("C", self.buf.at[z, y, x, :, pl.ds(c0, w)], [dev(z, y, x + d) for d in (2, 1, 3)])
+                along = (1, 0) if self.turned else (0, 1)
+                self.direct(
+                    "C", self.buf.at[z, y, x, :, pl.ds(c0, w)],
+                    [dev(z, y + d * along[0], x + d * along[1]) for d in (2, 1, 3)],
+                )
             elif k == 1:
                 self.wait("C")
-                block = self.at("C", pl.ds(z, 1), pl.ds(y, 1), pl.ds(0, NX))
-                self.direct("C", block, [dev(z, y + d, x) for d in (2, 1, 3)])
+                along = (0, 1) if self.turned else (1, 0)
+                plane = (pl.ds(0, NY), pl.ds(x, 1)) if self.turned else (pl.ds(y, 1), pl.ds(0, NX))
+                self.direct(
+                    "C", self.at("C", pl.ds(z, 1), *plane),
+                    [dev(z, y + d * along[0], x + d * along[1]) for d in (2, 1, 3)],
+                )
             else:
                 if k in (2, 6):
                     self.wait("C")

time: 68 us -> 65.7 us (0.966)
  Pallas kernels: 65.3 us -> 63 us
    pallas_call x1, Pallas kernels: 65.3 us -> 63 us  [body(): pl.pallas_call(kernel, out_shape=(jax.ShapeDtypeStruct((KMAX * ACTIONS, P...]
where the time goes in v3:
time: 65.7 us; the launch traced here: 65.6 us
  Pallas kernels  63 us (96%)
  local copies, waits for them, and re-layouts  1.89 us (3%)
    pallas_call x1, Pallas kernels, body(): pl.pallas_call(kernel, out_shape=(jax.ShapeDtypeStruct((KMAX * ACTIONS, P...  63 us
    unnamed x4, local copies, waits for them, and re-layouts  1.89 us

profile of v3, /device:TPU:1, one launch (start us, length us, event | category | flops | bytes accessed | tf_op | source)
XLA Modules:
  0.0 65.6 jit_solution(17967327162818880518)
XLA Ops:
  0.6 63.0 %shard_map.158 = (f32[32,192]{1,0:T(8,128)}, f32[1,48]{1,0:T(1,128)}) custom-call(bf16[192,1024]{1,0:T(8,128)(2,1)} %refs_0_.1, bf16[128,1024]{1,0:T(8,128)(2,1)} %refs_1_.1, bf16[256,1024]{1,0:T(8,128)(2,1)} %refs_2_.1, bf16[4,2048]{1,0:T(4,128)(2,1)} %refs_3_.1, f32[1,2048]{1,0:T(1,128)} %bitcast.15, bf16[8,2048]{1,0:T(8,128)(2,1)} %refs_5_.1, ...), custom_call_target="tpu_custom_call" | custom-call | tf_op jit(solution)/shard_map/pallas_call | solution.py:391
  63.7 0.0 copy-start
  63.7 1.4 %copy.19 = f32[192,32]{0,1:T(8,128)} copy(f32[192,32]{0,1:T(8,128)} %bitcast.14) | data formatting | bytes 49152
  65.1 0.0 copy-done
  65.1 0.5 copy.20
Async XLA Ops:
  63.7 1.4 %copy-start = (f32[1,48]{1,0:T(1,128)S(1)}, f32[1,48]{1,0:T(1,128)}, u32[]{:S(2)}) copy-start(f32[1,48]{1,0:T(1,128)} %get-tuple-element.5) | copy-start | bytes 580
